TPU v7x, 256 devices: a whole 4x4x8 slice. The times are simulated.
256 devices in a mesh: section: 32 (over x, z_lo, core), tensor: 8 (over z_hi, y).
Axes of the slice: x: 4, y: 4, z: 8 (z_hi: 2, z_lo: 4; z = z_hi * 4 + z_lo), core: 2. Of those that a mesh axis runs over, the one named last changes fastest.
Arguments:
- activations: bfloat16 [32, 256, 4096], P('section', 'tensor'), may hold values from -6 to 6
- upstream_grad: bfloat16 [32, 256, 4096], P('section', 'tensor'), may hold values from -6 to 6
- stash_blocks: bfloat16 [32, 256, 4096], P('section', 'tensor'), may hold values from -6 to 6
- guest_blocks: bfloat16 [32, 256, 4096], P('section', 'tensor'), may hold values from -6 to 6
- norm_gain: float32 [32, 4096], P('section'), may hold values from 0.1 to 1.9
- query_weight: bfloat16 [32, 4096, 4096], P('section', None, 'tensor'), may hold values from -2 to 2
- keyval_weight: bfloat16 [32, 4096, 2, 1024], P('section', None, None, 'tensor'), may hold values from -1 to 1
- output_weight: bfloat16 [32, 4096, 4096], P('section', 'tensor'), may hold values from -0.09375 to 0.09375
- evict_marks: int32 [32, 16], replicated, may hold values from 0 to 1, as said below
Outputs:
- next_input: bfloat16 [32, 256, 4096], P('section', 'tensor')
- prev_grad: bfloat16 [32, 256, 4096], P('section', 'tensor')
- kept_stash: bfloat16 [32, 256, 4096], P('section', 'tensor')
- held_blocks: bfloat16 [32, 256, 4096], P('section', 'tensor')
Inputs may be any that keep to these rules, and one draw needn't show every extreme that they name: `evict_marks`: row s marks with 1 the blocks that section s evicts to section 31 - s; a row has at most 8 ones, row 0 exactly 8, rows of the first half of the sections at least 4.
All inputs are finite; a program needn't handle non-finite values.
Results may differ from a plain program's by a relative error of at most 0.012.
Values may be sent and summed in bfloat16 or wider, within the bound.
A program may use at most 64 MiB of HBM per device.

v0:
```python
import jax
import jax.numpy as jnp
from jax import lax
from jax.sharding import PartitionSpec as P

HEADS = 32
KV_HEADS = 8
HEAD_DIM = 128


EPSILON = 1e-05
NEG_LARGE = -1e30


def from_partner(x, axis, bit):
    return lax.ppermute(x, axis, [(i, i ^ 1 << bit) for i in range(lax.axis_size(axis))])


def shifted(x, axis, by):
    peers = lax.axis_size(axis)
    pairs = [(i, i + by) for i in range(peers) if 0 <= i + by < peers]
    return lax.ppermute(x, axis, pairs)


def root_norm(features, gain_row):
    values = features.astype(jnp.float32)
    factor = lax.rsqrt(jnp.mean(values * values, axis=-1, keepdims=True) + EPSILON)
    return values * factor * gain_row


def causal_probs(scores):
    length = scores.shape[-1]
    allowed = jnp.arange(length)[:, None] >= jnp.arange(length)[None, :]
    masked = jnp.where(allowed, scores, NEG_LARGE)
    row_max = jnp.max(masked, axis=-1, keepdims=True)
    raised = jnp.exp(masked - row_max)
    return raised / jnp.sum(raised, axis=-1, keepdims=True)


def local(
    activations,
    upstream_grad,
    stash_blocks,
    guest_blocks,
    norm_gain,
    query_weight,
    keyval_weight,
    output_weight,
    evict_marks,
):
    sections = lax.axis_size("section")
    section_index = lax.axis_index("section")
    current = activations[0]
    upstream = upstream_grad[0]
    stash_rows = stash_blocks[0]
    guest_rows = guest_blocks[0]
    row_count, model_width = current.shape
    block_count = evict_marks.shape[1]
    block_rows = row_count // block_count
    own_marks = lax.dynamic_index_in_dim(evict_marks, section_index, 0, keepdims=False)
    own_mask = (jnp.repeat(own_marks, block_rows) == 1)[:, None]
    leaving = jnp.where(own_mask, current, jnp.zeros_like(current))
    payload = jnp.stack([guest_rows, leaving])
    bit_total = sections.bit_length() - 1
    bit_order = list(range(bit_total))
    for bit_number in bit_order:
        payload = from_partner(payload, "section", bit_number)
    returned = payload[0]
    arrived = payload[1]
    back_rows = jnp.where(own_mask, returned, stash_rows)
    kept_rows = jnp.where(own_mask, jnp.zeros_like(current), current)
    gain_row = norm_gain[0]
    query_local = query_weight[0]
    keyval_local = keyval_weight[0]
    output_local = output_weight[0]
    query_width = query_local.shape[1]
    keyval_width = keyval_local.shape[2]
    local_kv_heads = keyval_width // HEAD_DIM
    group_size = HEADS // KV_HEADS
    head_scale = HEAD_DIM ** (-0.5)
    keyval_flat = keyval_local.reshape(model_width, 2 * keyval_width)
    normed_now = root_norm(current, gain_row).astype(jnp.bfloat16)
    normed_back = root_norm(back_rows, gain_row).astype(jnp.bfloat16)
    stacked = jnp.stack([normed_now, normed_back, upstream], axis=1)
    fragment = lax.all_gather(stacked, "tensor", axis=0, tiled=True)
    outputs = [
        jnp.dot(fragment[:, 0], query_local, preferred_element_type=jnp.float32),
        jnp.dot(fragment[:, 0], keyval_flat, preferred_element_type=jnp.float32),
        jnp.dot(fragment[:, 1], query_local, preferred_element_type=jnp.float32),
        jnp.dot(fragment[:, 1], keyval_flat, preferred_element_type=jnp.float32),
        jnp.einsum("rd,cd->rc", fragment[:, 2], output_local, preferred_element_type=jnp.float32),
    ]
    projected = jnp.concatenate([result.astype(jnp.bfloat16) for result in outputs], axis=1)
    length = projected.shape[0]
    edge_two = query_width + 2 * keyval_width
    edge_three = edge_two + query_width
    edge_four = edge_three + 2 * keyval_width
    query_now = projected[:, :query_width].reshape(length, local_kv_heads, group_size, HEAD_DIM)
    keyval_now = projected[:, query_width:edge_two].reshape(length, 2, local_kv_heads, HEAD_DIM)
    query_back = projected[:, edge_two:edge_three].reshape(
        length, local_kv_heads, group_size, HEAD_DIM
    )
    keyval_back = projected[:, edge_three:edge_four].reshape(length, 2, local_kv_heads, HEAD_DIM)
    grad_context = projected[:, edge_four:].reshape(length, local_kv_heads, group_size, HEAD_DIM)
    scores_now = jnp.einsum(
        "tkgh,ukh->kgtu", query_now, keyval_now[:, 0], preferred_element_type=jnp.float32
    )
    probs_now = causal_probs(scores_now * head_scale)
    weights_now = probs_now.astype(jnp.bfloat16)
    context_now = jnp.einsum(
        "kgtu,ukh->tkgh", weights_now, keyval_now[:, 1], preferred_element_type=jnp.float32
    )
    context_flat = context_now.astype(jnp.bfloat16).reshape(length, query_width)
    key_back = keyval_back[:, 0]
    value_back = keyval_back[:, 1]
    scores_back = jnp.einsum(
        "tkgh,ukh->kgtu", query_back, key_back, preferred_element_type=jnp.float32
    )
    probs_back = causal_probs(scores_back * head_scale)
    weights_back = probs_back.astype(jnp.bfloat16)
    grad_value = jnp.einsum(
        "kgtu,tkgh->ukh", weights_back, grad_context, preferred_element_type=jnp.float32
    ).astype(jnp.bfloat16)
    grad_prob = jnp.einsum(
        "tkgh,ukh->kgtu", grad_context, value_back, preferred_element_type=jnp.float32
    )
    grad_score = (
        probs_back
        * (grad_prob - jnp.sum(probs_back * grad_prob, axis=-1, keepdims=True))
        * head_scale
    )
    grad_score = grad_score.astype(jnp.bfloat16)
    grad_query = jnp.einsum(
        "kgtu,ukh->tkgh", grad_score, key_back, preferred_element_type=jnp.float32
    )
    grad_query = grad_query.astype(jnp.bfloat16).reshape(length, query_width)
    grad_key = jnp.einsum(
        "kgtu,tkgh->ukh", grad_score, query_back, preferred_element_type=jnp.float32
    ).astype(jnp.bfloat16)
    grad_keyval = jnp.stack([grad_key, grad_value], axis=1).reshape(length, 2, keyval_width)
    forward_term = jnp.dot(context_flat, output_local, preferred_element_type=jnp.float32)
    backward_term = jnp.einsum(
        "tc,dc->td", grad_query, query_local, preferred_element_type=jnp.float32
    )
    backward_term = backward_term + jnp.einsum(
        "tjc,djc->td", grad_keyval, keyval_local, preferred_element_type=jnp.float32
    )
    rounded = lax.optimization_barrier(
        jnp.stack([forward_term, backward_term], axis=1).astype(jnp.bfloat16)
    )
    summed = lax.psum(rounded.astype(jnp.float32).astype(jnp.bfloat16), "tensor").astype(
        jnp.float32
    )
    own_share = lax.dynamic_slice_in_dim(summed, lax.axis_index("tensor") * row_count, row_count, 0)
    updated = (current.astype(jnp.float32) + own_share[:, 0]).astype(jnp.bfloat16)
    normed_out, pull_back = jax.vjp(
        lambda inputs: root_norm(inputs, gain_row), back_rows.astype(jnp.float32)
    )
    norm_grad = pull_back(own_share[:, 1])[0]
    passed = (upstream.astype(jnp.float32) + norm_grad).astype(jnp.bfloat16)
    sent_forward = shifted(updated[None], "section", 1)
    sent_back = shifted(passed[None], "section", -1)
    return (sent_forward, sent_back, kept_rows[None], arrived[None])


def solution(mesh):
    placed = (
        P("section", "tensor", None),
        P("section", "tensor", None),
        P("section", "tensor", None),
        P("section", "tensor", None),
        P("section", None),
        P("section", None, "tensor"),
        P("section", None, None, "tensor"),
        P("section", "tensor", None),
        P(),
    )
    return jax.shard_map(
        local,
        mesh=mesh,
        in_specs=placed,
        out_specs=(
            P("section", "tensor", None),
            P("section", "tensor", None),
            P("section", "tensor", None),
            P("section", "tensor", None),
        ),
        check_vma=False,
    )
```

profile of v0, /device:TPU:1, one launch (start us, length us, event | category | flops | bytes accessed | tf_op | source)
XLA Modules:
  0.0 462.8 jit_solution(203770623586910261)
XLA Ops:
  7.2 0.0 all-gather.2.cloned.1.call-start
  7.2 0.9 fusion.65
  8.1 0.1 broadcast_in_dim.52
  8.2 0.1 eq.20
  8.3 1.8 broadcast_select_fusion
  10.0 1.0 pad_maximum_fusion.2
  11.0 3.3 collective-permute-start
  14.3 1.5 collective-permute-done
  15.9 13.1 %collective-permute-done.1 = bf16[2,32,4096]{2,1,0:T(8,128)(2,1)S(1)} collective-permute-done((bf16[2,32,4096]{2,1,0:T(8,128)(2,1)S(1)}, bf16[2,32,4096]{2,1,0:T(8,128)(2,1)S(1)}, u32[]{:S(2)}, u32[]{:S(2)}) %collective-permute-start.1) | collective-permute-done | bytes 524320 | tf_op jit(solution)/shard_map/ppermute | solution.py:16
  29.0 1.6 collective-permute-start.2
  30.6 24.1 %collective-permute-done.2 = bf16[2,32,4096]{2,1,0:T(8,128)(2,1)S(1)} collective-permute-done((bf16[2,32,4096]{2,1,0:T(8,128)(2,1)S(1)}, bf16[2,32,4096]{2,1,0:T(8,128)(2,1)S(1)}, u32[]{:S(2)}, u32[]{:S(2)}) %collective-permute-start.2) | collective-permute-done | bytes 524320 | tf_op jit(solution)/shard_map/ppermute | solution.py:16
  54.7 0.0 collective-permute-start.3
  54.7 12.7 %collective-permute-done.3 = bf16[2,32,4096]{2,1,0:T(8,128)(2,1)S(1)} collective-permute-done((bf16[2,32,4096]{2,1,0:T(8,128)(2,1)S(1)}, bf16[2,32,4096]{2,1,0:T(8,128)(2,1)S(1)}, u32[]{:S(2)}, u32[]{:S(2)}) %collective-permute-start.3) | collective-permute-done | bytes 524320 | tf_op jit(solution)/shard_map/ppermute | solution.py:16
  67.4 0.5 collective-permute-start.4
  67.9 1.1 fusion.49
  69.0 11.7 %collective-permute-done.4 = bf16[2,32,4096]{2,1,0:T(8,128)(2,1)S(1)} collective-permute-done((bf16[2,32,4096]{2,1,0:T(8,128)(2,1)S(1)}, bf16[2,32,4096]{2,1,0:T(8,128)(2,1)S(1)}, u32[]{:S(2)}, u32[]{:S(2)}) %collective-permute-start.4) | collective-permute-done | bytes 524320 | tf_op jit(solution)/shard_map/ppermute | solution.py:16
  80.8 1.2 fusion.47
  82.0 1.3 fusion.53
  83.3 1.9 pad_maximum_fusion.1
  85.2 0.0 all-gather.2.cloned.1.call-update
  85.2 0.2 all-reduce.2.cloned.1.call-start
  85.5 141.2 %all-gather.2.cloned.1.call-done = bf16[256,3,4096]{2,0,1:T(8,128)(2,1)} async-done(((bf16[32,3,4096]{2,0,1:T(8,128)(2,1)}), bf16[256,3,4096]{2,0,1:T(8,128)(2,1)}) %all-gather.2.cloned.1.call-update) | async-done | bytes 6291472 | tf_op jit(solution)/shard_map/all_gather | solution.py:85
  226.6 4.1 fusion.25
  230.7 0.1 copy.55
  230.8 0.0 copy-start.4
  230.8 4.3 fusion.28
  235.1 0.1 copy.56
  235.3 2.5 fusion.37
  237.8 0.3 fusion.69
  238.1 0.2 fusion.46
  238.3 0.0 slice-start
  238.3 0.3 fusion.42
  238.7 0.0 slice-start.1
  238.7 0.3 multiply_reduce_fusion
  239.0 0.3 fusion.56
  239.3 0.0 copy-start.2
  239.3 0.3 fusion.43
  239.6 0.2 convolution_convert_fusion.1
  239.9 0.6 slice-done
  240.5 0.8 slice-done.1
  241.3 1.0 fusion.34
  242.3 0.3 copy-done.2
  242.6 1.3 fusion.31
  243.9 0.0 copy-start
  243.9 0.3 fusion.70
  244.3 0.2 fusion.44
  244.4 0.3 convolution_convert_fusion.2
  244.8 1.3 copy-done
  246.1 1.3 fusion.1
  247.4 0.8 convolution_bitcast_fusion
  248.2 1.3 fusion.2
  249.5 2.3 pad_maximum_fusion
  251.8 0.0 all-reduce.2.cloned.1.call-update
  251.9 190.3 %all-reduce.2.cloned.1.call-done = bf16[256,2,4096]{2,0,1:T(8,128)(2,1)} async-done(((bf16[256,2,4096]{2,0,1:T(8,128)(2,1)}), bf16[256,2,4096]{2,0,1:T(8,128)(2,1)}) %all-reduce.2.cloned.1.call-update) | async-done | bytes 4194320 | tf_op jit(solution)/shard_map/psum | solution.py:151
  442.1 1.1 dynamic-slice_convert_fusion
  443.3 0.3 fusion.48
  443.6 0.3 fusion.55
  443.9 2.5 collective-permute-start.6
  446.4 4.8 %collective-permute-start.5 = (bf16[1,32,4096]{2,1,0:T(8,128)(2,1)S(1)}, bf16[1,32,4096]{2,1,0:T(8,128)(2,1)S(1)}, u32[]{:S(2)}, u32[]{:S(2)}) collective-permute-start(bf16[1,32,4096]{2,1,0:T(8,128)(2,1)S(1)} %get-tuple-element.5), channel_id=1, source_target_pairs={{0,8},{8,16},{16,24},{24,32},{32,40},{40,48},{48,56},{56,64},{64,7... | collective-permute-start | bytes 786440 | tf_op jit(solution)/shard_map/ppermute | solution.py:22
  451.3 0.7 slice.56
  452.0 1.4 collective-permute-done.6
  453.4 1.2 collective-permute-done.5
  454.6 0.7 copy.82
  455.3 0.7 copy.83
  (15 shorter events, 0.1 us)
Async XLA Ops:
  7.2 219.5 %all-gather.2.cloned.1.call-start = ((), (), s32[]{:S(2)}) async-start(), calls=%async_computation | async-start | bytes 7077888 | tf_op jit(solution)/shard_map/all_gather | solution.py:85
  11.0 4.8 %collective-permute-start = (bf16[2,32,4096]{2,1,0:T(8,128)(2,1)S(1)}, bf16[2,32,4096]{2,1,0:T(8,128)(2,1)S(1)}, u32[]{:S(2)}, u32[]{:S(2)}) collective-permute-start(bf16[2,32,4096]{2,1,0:T(8,128)(2,1)S(1)} %pad_maximum_fusion.2), channel_id=1, source_target_pairs={{0,8},{8,0},{16,24},{24,16},{32,40},{40,32},{48,56},{56,48},{64,72... | collective-permute-start | bytes 1572872 | tf_op jit(solution)/shard_map/ppermute | solution.py:16
  15.9 13.1 %collective-permute-start.1 = (bf16[2,32,4096]{2,1,0:T(8,128)(2,1)S(1)}, bf16[2,32,4096]{2,1,0:T(8,128)(2,1)S(1)}, u32[]{:S(2)}, u32[]{:S(2)}) collective-permute-start(bf16[2,32,4096]{2,1,0:T(8,128)(2,1)S(1)} %collective-permute-done), channel_id=1, source_target_pairs={{0,16},{8,24},{16,0},{24,8},{32,48},{40,56},{48,32},{56,40},{64,80... | collective-permute-start | bytes 1572872 | tf_op jit(solution)/shard_map/ppermute | solution.py:16
  29.0 25.7 %collective-permute-start.2 = (bf16[2,32,4096]{2,1,0:T(8,128)(2,1)S(1)}, bf16[2,32,4096]{2,1,0:T(8,128)(2,1)S(1)}, u32[]{:S(2)}, u32[]{:S(2)}) collective-permute-start(bf16[2,32,4096]{2,1,0:T(8,128)(2,1)S(1)} %collective-permute-done.1), channel_id=1, source_target_pairs={{0,32},{8,40},{16,48},{24,56},{32,0},{40,8},{48,16},{56,24},{64,96... | collective-permute-start | bytes 1572872 | tf_op jit(solution)/shard_map/ppermute | solution.py:16
  54.7 12.7 %collective-permute-start.3 = (bf16[2,32,4096]{2,1,0:T(8,128)(2,1)S(1)}, bf16[2,32,4096]{2,1,0:T(8,128)(2,1)S(1)}, u32[]{:S(2)}, u32[]{:S(2)}) collective-permute-start(bf16[2,32,4096]{2,1,0:T(8,128)(2,1)S(1)} %collective-permute-done.2), channel_id=1, source_target_pairs={{0,64},{8,72},{16,80},{24,88},{32,96},{40,104},{48,112},{56,120},{... | collective-permute-start | bytes 1572872 | tf_op jit(solution)/shard_map/ppermute | solution.py:16
  67.4 13.4 %collective-permute-start.4 = (bf16[2,32,4096]{2,1,0:T(8,128)(2,1)S(1)}, bf16[2,32,4096]{2,1,0:T(8,128)(2,1)S(1)}, u32[]{:S(2)}, u32[]{:S(2)}) collective-permute-start(bf16[2,32,4096]{2,1,0:T(8,128)(2,1)S(1)} %collective-permute-done.3), channel_id=1, source_target_pairs={{0,128},{8,136},{16,144},{24,152},{32,160},{40,168},{48,176},{56,1... | collective-permute-start | bytes 1572872 | tf_op jit(solution)/shard_map/ppermute | solution.py:16
  85.2 356.9 %all-reduce.2.cloned.1.call-start = ((), (), s32[]{:S(2)}) async-start(), calls=%async_computation.1 | async-start | bytes 8388608 | tf_op jit(solution)/shard_map/psum | solution.py:151
  230.8 4.4 copy-start.4
  238.3 2.2 slice-start
  238.7 2.6 slice-start.1
  239.3 3.3 copy-start.2
  243.9 2.2 copy-start
  251.8 191.4 %copy-start.1 = (bf16[1,32,4096]{2,1,0:T(8,128)(2,1)S(1)}, bf16[1,32,4096]{2,1,0:T(8,128)(2,1)}, u32[]{:S(2)}) copy-start(bf16[1,32,4096]{2,1,0:T(8,128)(2,1)} %param.11) | copy-start | bytes 786436
  251.8 191.4 %copy-start.6 = (f32[1,4096]{1,0:T(1,128)S(1)}, f32[1,4096]{1,0:T(1,128)}, u32[]{:S(2)}) copy-start(f32[1,4096]{1,0:T(1,128)} %param.13) | copy-start | bytes 49156
  251.8 191.8 %copy-start.3 = (bf16[1,32,4096]{2,1,0:T(8,128)(2,1)S(1)}, bf16[1,32,4096]{2,1,0:T(8,128)(2,1)}, u32[]{:S(2)}) copy-start(bf16[1,32,4096]{2,1,0:T(8,128)(2,1)} %param.9) | copy-start | bytes 786436
  251.8 191.8 %copy-start.5 = (bf16[1,32,4096]{2,1,0:T(8,128)(2,1)S(1)}, bf16[1,32,4096]{2,1,0:T(8,128)(2,1)}, u32[]{:S(2)}) copy-start(bf16[1,32,4096]{2,1,0:T(8,128)(2,1)} %param.10) | copy-start | bytes 786436
  443.9 9.5 %collective-permute-start.6 = (bf16[1,32,4096]{2,1,0:T(8,128)(2,1)S(1)}, bf16[1,32,4096]{2,1,0:T(8,128)(2,1)S(1)}, u32[]{:S(2)}, u32[]{:S(2)}) collective-permute-start(bf16[1,32,4096]{2,1,0:T(8,128)(2,1)S(1)} %get-tuple-element.4), channel_id=1, source_target_pairs={{8,0},{16,8},{24,16},{32,24},{40,32},{48,40},{56,48},{64,56},{72,6... | collective-permute-start | bytes 786440 | tf_op jit(solution)/shard_map/ppermute | solution.py:22
  446.4 8.1 %collective-permute-start.5 = (bf16[1,32,4096]{2,1,0:T(8,128)(2,1)S(1)}, bf16[1,32,4096]{2,1,0:T(8,128)(2,1)S(1)}, u32[]{:S(2)}, u32[]{:S(2)}) collective-permute-start(bf16[1,32,4096]{2,1,0:T(8,128)(2,1)S(1)} %get-tuple-element.5), channel_id=1, source_target_pairs={{0,8},{8,16},{16,24},{24,32},{32,40},{40,48},{48,56},{56,64},{64,7... | collective-permute-start | bytes 786440 | tf_op jit(solution)/shard_map/ppermute | solution.py:22
Sparse Core Ops, SparseCore 0:
  85.3 141.2 all-gather.1
  252.0 190.1 all-reduce.1
where the time goes:
time: 466 us; the launch traced here: 463 us
  waiting for transfers between devices  397 us (85%)
  matrix products  18.8 us (4%)
  between operations  14.3 us (3%)
  other arithmetic  13.8 us (3%)
  starting transfers between devices  13.1 us (3%)
  local copies, waits for them, and re-layouts  5.6 us (1%)
    psum x1, waiting for transfers between devices, local(): lax.psum(rounded.astype(jnp.float32).astype(jnp.bfloat16), 'tensor')  190 us
    all_gather x1, waiting for transfers between devices, local(): fragment = lax.all_gather(stacked, 'tensor', axis=0, tiled=True)  141 us
    ppermute x5, waiting for transfers between devices, from_partner(): lax.ppermute(x, axis, [(i, i ^ 1 << bit) for i in range(lax.axis_size(axi...  63.1 us
  transfers between devices with their start and end apart: 9, of which 9 were waited for; matrix products, arithmetic and copies ran while one was open for 0% of the time, Pallas kernels for 0%

commit v1 on v0

v1 whole, which is shorter than its diff:
```python
import jax
import jax.numpy as jnp
from jax import lax
from jax.experimental import pallas as pl
from jax.experimental.pallas import tpu as pltpu
from jax.sharding import PartitionSpec as P

HEADS = 32
KV_HEADS = 8
HEAD_DIM = 128
GROUP = HEADS // KV_HEADS
EPSILON = 1e-05
NEG_LARGE = -1e30
MESH = pl.DeviceIdType.MESH
F32 = jnp.float32
BF16 = jnp.bfloat16

ROWS = 32
WIDTH = 4096
HALF = WIDTH // 2
BLOCKS = 16
PACKED = 16
CHUNKS = 2
CHUNK = ROWS // CHUNKS
QCOLS = 512
CCOLS = 768
LENGTH = 256
NOW, UP, BACK = 0, 1, 2


def copy_numbers():
    names = []
    for tensor in range(3):
        names.append(("z", tensor))
        for tag in range(2):
            for way in range(2):
                names.append(("y", tensor, tag, way))
                names.append(("half", tensor, tag, way))
    for total in range(2):
        for chunk in range(CHUNKS):
            for tag in range(2):
                for way in range(2):
                    names.append(("part", total, chunk, tag, way))
                    names.append(("pair", total, chunk, tag, way))
            names.append(("sum", total, chunk))
            names.append(("shift", total, chunk))
    names.append(("guest",))
    names.append(("leave",))
    return {name: number for number, name in enumerate(names)}


COPIES = copy_numbers()


def dot(left, right):
    return jnp.dot(left, right, preferred_element_type=F32)


def dot_last(left, right):
    return lax.dot_general(left, right, (((1,), (1,)), ((), ())), preferred_element_type=F32)


def dot_first(left, right):
    return lax.dot_general(left, right, (((0,), (0,)), ((), ())), preferred_element_type=F32)


def iota(shape, axis):
    return lax.broadcasted_iota(jnp.int32, shape, axis)


def relay_kernel(
    act_in,
    up_in,
    stash_in,
    guest_in,
    gain_in,
    query_in,
    keyval_in,
    output_in,
    marks_in,
    next_out,
    prev_out,
    held_out,
    kept_out,
    gath,
    part,
    halves,
    pairs,
    zsend,
    zrecv,
    act_v,
    stash_v,
    guest_v,
    back_v,
    gain_v,
    marks_v,
    kv_mixed,
    wcat,
    wout,
    qkv,
    context,
    gctx,
    gcat,
    pack_send,
    pack_recv,
    kept_v,
    held_v,
    shift_v,
    send_sem,
    recv_sem,
    local_sem,
):
    section = lax.axis_index("section")
    tensor = lax.axis_index("tensor")
    plane = tensor // 4
    y = tensor % 4
    sections = 32
    y_up = (y + 1) % 4
    y_down = (y + 3) % 4
    y_far = (y + 2) % 4

    def at(section_to, tensor_to):
        return {"section": section_to, "tensor": tensor_to}

    to_up = at(section, plane * 4 + y_up)
    to_down = at(section, plane * 4 + y_down)
    to_far_z = at(section, (1 - plane) * 4 + y)
    to_mirror = at(sections - 1 - section, tensor)
    to_next = at((section + 1) % sections, tensor)
    to_prev = at((section + sections - 1) % sections, tensor)
    peers = (to_up, to_down, to_far_z, to_mirror, to_next, to_prev)

    barrier = pltpu.get_barrier_semaphore()
    for peer in peers:
        pl.semaphore_signal(barrier, inc=1, device_id=peer, device_id_type=MESH)

    local = {}
    for number, (name, source, target) in enumerate(
        (
            ("up", up_in, gath.at[UP, plane, y]),
            ("act", act_in, act_v),
            ("gain", gain_in, gain_v),
            ("marks", marks_in, marks_v),
            ("guest", guest_in, guest_v),
            ("stash", stash_in, stash_v),
            ("keyval", keyval_in, kv_mixed),
            ("query", query_in, wcat.at[:, pl.ds(0, QCOLS)]),
            ("output", output_in, wout),
        )
    ):
        local[name] = pltpu.make_async_copy(source, target, local_sem.at[number])
        local[name].start()

    sends = []

    def remote(name, source, target, device):
        number = COPIES[name]
        return pltpu.make_async_remote_copy(
            src_ref=source,
            dst_ref=target,
            send_sem=send_sem.at[number],
            recv_sem=recv_sem.at[number],
            device_id=device,
            device_id_type=MESH,
        )

    def send(name, source, target, device):
        copy = remote(name, source, target, device)
        copy.start()
        sends.append(copy)

    def receive(name, target):
        remote(name, target, target, to_up).wait_recv()

    planes = (plane, 1 - plane)
    ways = ((to_up, y_down, 0), (to_down, y_up, HALF))

    def gather_z(which):
        ref = gath.at[which, plane, y]
        send(("z", which), ref, ref, to_far_z)

    def gather_z_done(which):
        receive(("z", which), gath.at[which, 1 - plane, y])

    def gather_y(which, tag):
        ref = gath.at[which, planes[tag], y]
        for way in range(2):
            send(("y", which, tag, way), ref, ref, ways[way][0])

    def gather_forward(which, tag):
        for way in range(2):
            target, source_y, column = ways[way]
            ref = gath.at[which, planes[tag], source_y]
            receive(("y", which, tag, way), ref)
            piece = ref.at[:, pl.ds(column, HALF)]
            send(("half", which, tag, way), piece, piece, target)

    def gather_done(which, tag):
        for way in range(2):
            column = ways[way][2]
            piece = gath.at[which, planes[tag], y_far, :, pl.ds(column, HALF)]
            receive(("half", which, tag, way), piece)

    def rows_of(chunk):
        return pl.ds(chunk * CHUNK, CHUNK)

    def sum_far(total, chunk, tag):
        for way in range(2):
            target, _, column = ways[way]
            piece = part.at[total, planes[tag], y_far, rows_of(chunk), pl.ds(column, HALF)]
            send(("part", total, chunk, tag, way), piece, halves.at[total, chunk, tag, way], target)

    def sum_near(total, chunk, tag):
        for way in range(2):
            target, _, column = ways[way]
            near = y_up if way == 0 else y_down
            landed = halves.at[total, chunk, tag, way]
            receive(("part", total, chunk, tag, way), landed)
            piece = (total, planes[tag], near, rows_of(chunk), pl.ds(column, HALF))
            part[piece] = (part[piece].astype(F32) + landed[...].astype(F32)).astype(BF16)
            send(
                ("pair", total, chunk, tag, way),
                part.at[total, planes[tag], near, rows_of(chunk)],
                pairs.at[total, chunk, tag, way],
                target,
            )

    def plane_sum(total, chunk, tag):
        for way in range(2):
            receive(("pair", total, chunk, tag, way), pairs.at[total, chunk, tag, way])
        own = part[total, planes[tag], y, rows_of(chunk)].astype(F32)
        return (
            own
            + pairs[total, chunk, tag, 0].astype(F32)
            + pairs[total, chunk, tag, 1].astype(F32)
        )

    def sum_cross(total, chunk):
        zsend[total, chunk] = plane_sum(total, chunk, 1).astype(BF16)
        send(("sum", total, chunk), zsend.at[total, chunk], zrecv.at[total, chunk], to_far_z)

    def sum_total(total, chunk):
        own = plane_sum(total, chunk, 0)
        receive(("sum", total, chunk), zrecv.at[total, chunk])
        return own + zrecv[total, chunk].astype(F32)

    def normed(values):
        factor = lax.rsqrt(jnp.mean(values * values, axis=-1, keepdims=True) + EPSILON)
        return (values * factor * gain_v[...]).astype(BF16)

    local["act"].wait()
    local["gain"].wait()
    gath[NOW, plane, y] = normed(act_v[...].astype(F32))
    local["up"].wait()
    pl.semaphore_wait(barrier, len(peers))
    gather_z(NOW)
    gather_y(UP, 0)
    gather_y(NOW, 0)

    local["marks"].wait()
    marked = jnp.where(marks_v[...] == 1, 1.0, 0.0).astype(BF16)
    spread = jnp.where(iota((ROWS, BLOCKS), 0) // 2 == iota((ROWS, BLOCKS), 1), 1.0, 0.0)
    row_marks = dot(spread.astype(BF16), marked)
    first = iota((ROWS, ROWS), 0)
    second = iota((ROWS, ROWS), 1)

    def selection(which_section):
        column = jnp.sum(jnp.where(second == which_section, row_marks, 0.0), axis=1, keepdims=True)
        wide = jnp.broadcast_to(column, (ROWS, ROWS))
        line = jnp.sum(jnp.where(first == second, wide, 0.0), axis=0, keepdims=True)
        line_rank = jnp.sum(jnp.where(first < second, wide, 0.0), axis=0, keepdims=True)
        tall = jnp.broadcast_to(line, (ROWS, ROWS))
        column_rank = jnp.sum(jnp.where(second < first, tall, 0.0), axis=1, keepdims=True)
        slot = iota((PACKED, ROWS), 0).astype(F32)
        pack = jnp.where(slot == line_rank, jnp.broadcast_to(line, (PACKED, ROWS)), 0.0)
        slot = iota((ROWS, PACKED), 1).astype(F32)
        unpack = jnp.where(slot == column_rank, jnp.broadcast_to(column, (ROWS, PACKED)), 0.0)
        return column > 0.5, pack.astype(BF16), unpack.astype(BF16)

    own_moved, own_pack, own_unpack = selection(section)
    far_moved, far_pack, far_unpack = selection(sections - 1 - section)
    local["guest"].wait()
    pack_send[0] = dot(far_pack, guest_v[...]).astype(BF16)
    send(("guest",), pack_send.at[0], pack_recv.at[0], to_mirror)
    gather_z(UP)
    pack_send[1] = dot(own_pack, act_v[...]).astype(BF16)
    send(("leave",), pack_send.at[1], pack_recv.at[1], to_mirror)
    kept_v[...] = jnp.where(own_moved, 0.0, act_v[...].astype(F32)).astype(BF16)
    kept_copy = pltpu.make_async_copy(kept_v, kept_out, local_sem.at[9])
    kept_copy.start()

    local["keyval"].wait()
    block = 2 * HEAD_DIM
    out_row = iota((block, block), 0)
    wanted = jnp.where(out_row < HEAD_DIM, 2 * out_row, 2 * (out_row - HEAD_DIM) + 1)
    sort_rows = jnp.where(iota((block, block), 1) == wanted, 1.0, 0.0).astype(BF16)

    def split_rows(step, carry):
        sorted_rows = dot(sort_rows, kv_mixed[pl.ds(pl.multiple_of(step * block, block), block), :])
        sorted_rows = sorted_rows.astype(BF16)
        target = pl.ds(pl.multiple_of(step * HEAD_DIM, HEAD_DIM), HEAD_DIM)
        wcat[target, QCOLS : QCOLS + HEAD_DIM] = sorted_rows[:HEAD_DIM]
        wcat[target, QCOLS + HEAD_DIM :] = sorted_rows[HEAD_DIM:]
        return carry

    lax.fori_loop(0, WIDTH // HEAD_DIM, split_rows, 0)

    gather_forward(UP, 0)
    local["stash"].wait()
    receive(("guest",), pack_recv.at[0])
    returned = dot(own_unpack, pack_recv[0])
    back_rows = jnp.where(own_moved, returned, stash_v[...].astype(F32))
    back_v[...] = back_rows.astype(BF16)
    gath[BACK, plane, y] = normed(back_rows)
    gather_y(BACK, 0)
    gather_z(BACK)
    gather_forward(NOW, 0)
    receive(("leave",), pack_recv.at[1])
    held_v[...] = dot(far_unpack, pack_recv[1]).astype(BF16)
    held_copy = pltpu.make_async_copy(held_v, held_out, local_sem.at[10])
    held_copy.start()
    gather_z_done(NOW)
    gather_y(NOW, 1)
    gather_forward(BACK, 0)
    gather_z_done(UP)
    gather_y(UP, 1)
    gather_forward(NOW, 1)
    gather_done(NOW, 0)
    gather_done(NOW, 1)
    local["query"].wait()

    def project(which):
        def tile(step, carry):
            columns = pl.ds(pl.multiple_of(step * 256, 256), 256)
            rows = gath[which].reshape(LENGTH, WIDTH)
            qkv[which // 2, :, columns] = dot(rows, wcat[:, columns]).astype(BF16)
            return carry

        lax.fori_loop(0, CCOLS // 256, tile, 0)

    scale = HEAD_DIM ** (-0.5)

    def probabilities(queries, keys):
        scores = dot_last(queries, keys) * scale
        allowed = iota((LENGTH, LENGTH), 0) >= iota((LENGTH, LENGTH), 1)
        masked = jnp.where(allowed, scores, NEG_LARGE)
        raised = jnp.exp(masked - jnp.max(masked, axis=-1, keepdims=True))
        return raised / jnp.sum(raised, axis=-1, keepdims=True)

    project(NOW)
    gather_z_done(BACK)
    gather_y(BACK, 1)
    gather_forward(UP, 1)

    keys_now = qkv[0, :, QCOLS : QCOLS + HEAD_DIM]
    values_now = qkv[0, :, QCOLS + HEAD_DIM :]
    for head in range(GROUP):
        columns = slice(head * HEAD_DIM, (head + 1) * HEAD_DIM)
        weights = probabilities(qkv[0, :, columns], keys_now).astype(BF16)
        context[:, columns] = dot(weights, values_now).astype(BF16)

    local["output"].wait()

    def forward_tile(step, carry):
        columns = pl.ds(pl.multiple_of(step * 512, 512), 512)
        result = dot(context[...], wout[:, columns]).astype(BF16)
        part[0, :, :, :, columns] = result.reshape(2, 4, ROWS, 512)
        return carry

    lax.fori_loop(0, WIDTH // 512, forward_tile, 0)

    gather_forward(BACK, 1)
    for chunk in range(CHUNKS):
        for tag in (1, 0):
            sum_far(0, chunk, tag)

    gather_done(UP, 0)
    gather_done(UP, 1)

    def grad_tile(step, carry):
        columns = pl.ds(pl.multiple_of(step * 256, 256), 256)
        rows = gath[UP].reshape(LENGTH, WIDTH)
        gctx[:, columns] = dot_last(rows, wout[columns, :]).astype(BF16)
        return carry

    lax.fori_loop(0, QCOLS // 256, grad_tile, 0)

    gather_done(BACK, 0)
    gather_done(BACK, 1)
    sum_near(0, 0, 1)
    sum_near(0, 0, 0)
    project(BACK)
    sum_near(0, 1, 1)
    sum_near(0, 1, 0)

    keys_back = qkv[1, :, QCOLS : QCOLS + HEAD_DIM]
    values_back = qkv[1, :, QCOLS + HEAD_DIM :]
    grad_key = jnp.zeros((LENGTH, HEAD_DIM), F32)
    grad_value = jnp.zeros((LENGTH, HEAD_DIM), F32)
    for head in range(GROUP):
        columns = slice(head * HEAD_DIM, (head + 1) * HEAD_DIM)
        queries = qkv[1, :, columns]
        grads = gctx[:, columns]
        probs = probabilities(queries, keys_back)
        grad_value = grad_value + dot_first(probs.astype(BF16), grads)
        grad_prob = dot_last(grads, values_back)
        inner = jnp.sum(probs * grad_prob, axis=-1, keepdims=True)
        grad_score = (probs * (grad_prob - inner) * scale).astype(BF16)
        gcat[:, columns] = dot(grad_score, keys_back).astype(BF16)
        grad_key = grad_key + dot_first(grad_score, queries)
    gcat[:, QCOLS : QCOLS + HEAD_DIM] = grad_key.astype(BF16)
    gcat[:, QCOLS + HEAD_DIM :] = grad_value.astype(BF16)

    sum_cross(0, 0)

    for chunk in range(CHUNKS):
        grads = gcat[...].reshape(8, ROWS, CCOLS)[:, chunk * CHUNK : (chunk + 1) * CHUNK]
        grads = grads.reshape(8 * CHUNK, CCOLS)

        def backward_tile(step, carry):
            columns = pl.ds(pl.multiple_of(step * 512, 512), 512)
            result = dot_last(grads, wcat[columns, :]).astype(BF16)
            part[1, :, :, rows_of(chunk), columns] = result.reshape(2, 4, CHUNK, 512)
            return carry

        lax.fori_loop(0, WIDTH // 512, backward_tile, 0)
        for tag in (1, 0):
            sum_far(1, chunk, tag)

    sum_cross(0, 1)

    def finish_forward(chunk):
        rows = rows_of(chunk)
        total = sum_total(0, chunk)
        shift_v[0, rows] = (act_v[rows, :].astype(F32) + total).astype(BF16)
        send(("shift", 0, chunk), shift_v.at[0, rows], next_out.at[rows], to_next)

    def finish_backward(chunk):
        rows = rows_of(chunk)
        values = back_v[rows, :].astype(F32)
        factor = lax.rsqrt(jnp.mean(values * values, axis=-1, keepdims=True) + EPSILON)
        upstream = gath[UP, plane, y, rows].astype(F32)
        grads = sum_total(1, chunk) * gain_v[...]
        inner = jnp.sum(grads * values, axis=-1, keepdims=True) * (factor * factor * factor)
        norm_grad = grads * factor - values * (inner * (1.0 / WIDTH))
        shift_v[1, rows] = (upstream + norm_grad).astype(BF16)
        send(("shift", 1, chunk), shift_v.at[1, rows], prev_out.at[rows], to_prev)

    sum_near(1, 0, 1)
    sum_near(1, 0, 0)
    finish_forward(0)
    sum_near(1, 1, 1)
    sum_near(1, 1, 0)
    finish_forward(1)
    sum_cross(1, 0)
    sum_cross(1, 1)
    finish_backward(0)
    finish_backward(1)

    kept_copy.wait()
    held_copy.wait()
    for copy in sends:
        copy.wait_send()
    for chunk in range(CHUNKS):
        receive(("shift", 0, chunk), next_out.at[rows_of(chunk)])
        receive(("shift", 1, chunk), prev_out.at[rows_of(chunk)])


def relay(act, up, stash, guest, gain, query, keyval, output, marks):
    block = jax.ShapeDtypeStruct((ROWS, WIDTH), BF16)
    anywhere = pl.BlockSpec(memory_space=pl.ANY)
    count = len(COPIES)
    vmem = pltpu.VMEM
    return pl.pallas_call(
        relay_kernel,
        out_shape=(block, block, block, block),
        in_specs=[anywhere] * 9,
        out_specs=(anywhere,) * 4,
        scratch_shapes=[
            vmem((3, 2, 4, ROWS, WIDTH), BF16),
            vmem((2, 2, 4, ROWS, WIDTH), BF16),
            vmem((2, CHUNKS, 2, 2, CHUNK, HALF), BF16),
            vmem((2, CHUNKS, 2, 2, CHUNK, WIDTH), BF16),
            vmem((2, CHUNKS, CHUNK, WIDTH), BF16),
            vmem((2, CHUNKS, CHUNK, WIDTH), BF16),
            vmem((ROWS, WIDTH), BF16),
            vmem((ROWS, WIDTH), BF16),
            vmem((ROWS, WIDTH), BF16),
            vmem((ROWS, WIDTH), BF16),
            vmem((1, WIDTH), F32),
            vmem((BLOCKS, 32), jnp.int32),
            vmem((2 * WIDTH, HEAD_DIM), BF16),
            vmem((WIDTH, CCOLS), BF16),
            vmem((QCOLS, WIDTH), BF16),
            vmem((2, LENGTH, CCOLS), BF16),
            vmem((LENGTH, QCOLS), BF16),
            vmem((LENGTH, QCOLS), BF16),
            vmem((LENGTH, CCOLS), BF16),
            vmem((2, PACKED, WIDTH), BF16),
            vmem((2, PACKED, WIDTH), BF16),
            vmem((ROWS, WIDTH), BF16),
            vmem((ROWS, WIDTH), BF16),
            vmem((2, ROWS, WIDTH), BF16),
            pltpu.SemaphoreType.DMA((count,)),
            pltpu.SemaphoreType.DMA((count,)),
            pltpu.SemaphoreType.DMA((11,)),
        ],
        compiler_params=pltpu.CompilerParams(
            collective_id=0, has_side_effects=True, vmem_limit_bytes=60 * 2**20
        ),
    )(act, up, stash, guest, gain, query, keyval, output, marks)


def local(
    activations,
    upstream_grad,
    stash_blocks,
    guest_blocks,
    norm_gain,
    query_weight,
    keyval_weight,
    output_weight,
    evict_marks,
):
    section = lax.axis_index("section")
    next_raw, prev_raw, held, kept = relay(
        activations[0],
        upstream_grad[0],
        stash_blocks[0],
        guest_blocks[0],
        norm_gain,
        query_weight[0],
        keyval_weight[0].reshape(2 * WIDTH, HEAD_DIM),
        output_weight[0],
        evict_marks.T,
    )
    next_input = jnp.where(section == 0, jnp.zeros_like(next_raw), next_raw)
    last = lax.axis_size("section") - 1
    prev_grad = jnp.where(section == last, jnp.zeros_like(prev_raw), prev_raw)
    return (next_input[None], prev_grad[None], kept[None], held[None])


def solution(mesh):
    placed = (
        P("section", "tensor", None),
        P("section", "tensor", None),
        P("section", "tensor", None),
        P("section", "tensor", None),
        P("section", None),
        P("section", None, "tensor"),
        P("section", None, None, "tensor"),
        P("section", "tensor", None),
        P(),
    )
    return jax.shard_map(
        local,
        mesh=mesh,
        in_specs=placed,
        out_specs=(P("section", "tensor", None),) * 4,
        check_vma=False,
    )
```

time: 466 us -> 142 us (0.30)
  waiting for transfers between devices: 397 us -> 0 us
  Pallas kernels: 0 us -> 136 us
  matrix products: 18.8 us -> 0 us
  between operations: 14.3 us -> 0.65 us
  starting transfers between devices: 13.1 us -> 0 us
  other arithmetic: 13.8 us -> 1.87 us
    psum x1 -> x0, waiting for transfers between devices: 190 us -> none  [local(): lax.psum(rounded.astype(jnp.float32).astype(jnp.bfloat16), 'tensor')]
    all_gather x1 -> x0, waiting for transfers between devices: 141 us -> none  [local(): fragment = lax.all_gather(stacked, 'tensor', axis=0, tiled=True)]
    pallas_call x0 -> x1, Pallas kernels: none -> 136 us  [relay(): pl.pallas_call(relay_kernel, out_shape=(block, block, block, block), in_s...]
    ppermute x7 -> x0, waiting for transfers between devices: 65.7 us -> none  [the longest x5 63.1 us: from_partner(): lax.ppermute(x, axis, [(i, i ^ 1 << bit) for i in range(lax.axis_size(axi...]
    dot_general x15 -> x0, matrix products: 18.8 us -> none  [the longest x1 4.26 us: local(): jnp.einsum('rd,cd->rc', fragment[:, 2], output_local, preferred_element_t...]
    ppermute x7 -> x0, starting transfers between devices: 12.8 us -> none  [the longest x2 7.38 us: shifted(): return lax.ppermute(x, axis, pairs)]
    another operation x4 -> x0, other arithmetic: 5.54 us -> none  [the longest x1 2.33 us: local(): jnp.stack([forward_term, backward_term], axis=1).astype(jnp.bfloat16)]
  transfers between devices with their start and end apart: 9 -> 0, of which waited for: 9 -> 0; matrix products, arithmetic and copies ran while one was open for 0% -> 0% of each run, Pallas kernels for 0% -> 0%
where the time goes in v1:
time: 142 us
  Pallas kernels  136 us (96%)
  local copies, waits for them, and re-layouts  3.34 us (2%)
  other arithmetic  1.87 us (1%)
    pallas_call x1, Pallas kernels, relay(): pl.pallas_call(relay_kernel, out_shape=(block, block, block, block), in_s...  136 us
    unnamed x2, local copies, waits for them, and re-layouts  3.34 us

profile of v1, /device:TPU:1, one launch (start us, length us, event | category | flops | bytes accessed | tf_op | source)
XLA Modules:
  0.0 142.1 jit_solution(4194238962617028221)
XLA Ops:
  0.6 136.2 %shard_map.120 = (bf16[32,4096]{1,0:T(8,128)(2,1)}, bf16[32,4096]{1,0:T(8,128)(2,1)}, bf16[32,4096]{1,0:T(8,128)(2,1)}, bf16[32,4096]{1,0:T(8,128)(2,1)}) custom-call(bf16[32,4096]{1,0:T(8,128)(2,1)} %bitcast.17, bf16[32,4096]{1,0:T(8,128)(2,1)} %bitcast.18, bf16[32,4096]{1,0:T(8,128)(2,1)} %bitcast.19, bf16[32,4096]{1,0:T(8,128)(2,1)} %bitcast.20, ...), custom_call_target="tpu_custom_call" | custom-call | tf_op jit(solution)/shard_map/pallas_call | solution.py:474
  136.9 1.9 %select_bitcast_fusion = (bf16[1,32,4096]{2,1,0:T(8,128)(2,1)}, bf16[1,32,4096]{2,1,0:T(8,128)(2,1)}) fusion(bf16[32,4096]{1,0:T(8,128)(2,1)} %get-tuple-element.9, pred[]{:T(512)S(6)} %eq.7, bf16[32,4096]{1,0:T(8,128)(2,1)} %get-tuple-element.8, pred[]{:T(512)S(6)} %eq.6), kind=kLoop, calls=%fused_computation | loop fusion | flops 262144 | bytes 1048578 | tf_op jit(solution)/shard_map/broadcast_in_dim | solution.py:540
  138.8 1.7 %copy.15 = bf16[1,32,4096]{2,1,0:T(8,128)(2,1)} copy(bf16[1,32,4096]{2,1,0:T(8,128)(2,1)} %bitcast.22) | data formatting | bytes 524288
  140.4 1.7 %copy.16 = bf16[1,32,4096]{2,1,0:T(8,128)(2,1)} copy(bf16[1,32,4096]{2,1,0:T(8,128)(2,1)} %bitcast.21) | data formatting | bytes 524288

commit v2 on v1

--- a/solution.py
+++ b/solution.py
@@ -18,10 +18,12 @@
 ROWS = 32
 WIDTH = 4096
 HALF = WIDTH // 2
+QUARTER = WIDTH // 4
 BLOCKS = 16
 PACKED = 16
-CHUNKS = 2
+CHUNKS = 4
 CHUNK = ROWS // CHUNKS
+STAGES = 2
 QCOLS = 512
 CCOLS = 768
 LENGTH = 256
@@ -31,11 +33,14 @@
 def copy_numbers():
     names = []
     for tensor in range(3):
-        names.append(("z", tensor))
-        for tag in range(2):
+        for way in range(2):
+            names.append(("own", tensor, way))
+            names.append(("own half", tensor, way))
+        for piece in range(2):
+            names.append(("z", tensor, piece))
             for way in range(2):
-                names.append(("y", tensor, tag, way))
-                names.append(("half", tensor, tag, way))
+                names.append(("far", tensor, piece, way))
+                names.append(("far half", tensor, piece, way))
     for total in range(2):
         for chunk in range(CHUNKS):
             for tag in range(2):
@@ -175,31 +180,52 @@
     planes = (plane, 1 - plane)
     ways = ((to_up, y_down, 0), (to_down, y_up, HALF))
 
-    def gather_z(which):
+    def columns_of(piece):
+        return pl.ds(piece * HALF, HALF)
+
+    def cross(which, piece):
+        ref = gath.at[which, plane, y, :, columns_of(piece)]
+        send(("z", which, piece), ref, ref, to_far_z)
+
+    def crossed(which, piece):
+        receive(("z", which, piece), gath.at[which, 1 - plane, y, :, columns_of(piece)])
+        ref = gath.at[which, 1 - plane, y, :, columns_of(piece)]
+        for way in range(2):
+            send(("far", which, piece, way), ref, ref, ways[way][0])
+
+    def far_forward(which, piece):
+        for way in range(2):
+            target, source_y, _ = ways[way]
+            ref = gath.at[which, 1 - plane, source_y]
+            receive(("far", which, piece, way), ref.at[:, columns_of(piece)])
+            part_ref = ref.at[:, pl.ds(piece * HALF + way * QUARTER, QUARTER)]
+            send(("far half", which, piece, way), part_ref, part_ref, target)
+
+    def far_done(which):
+        for piece in range(2):
+            for way in range(2):
+                columns = pl.ds(piece * HALF + way * QUARTER, QUARTER)
+                receive(
+                    ("far half", which, piece, way), gath.at[which, 1 - plane, y_far, :, columns]
+                )
+
+    def own_send(which):
         ref = gath.at[which, plane, y]
-        send(("z", which), ref, ref, to_far_z)
-
-    def gather_z_done(which):
-        receive(("z", which), gath.at[which, 1 - plane, y])
-
-    def gather_y(which, tag):
-        ref = gath.at[which, planes[tag], y]
-        for way in range(2):
-            send(("y", which, tag, way), ref, ref, ways[way][0])
-
-    def gather_forward(which, tag):
+        for way in range(2):
+            send(("own", which, way), ref, ref, ways[way][0])
+
+    def own_forward(which):
         for way in range(2):
             target, source_y, column = ways[way]
-            ref = gath.at[which, planes[tag], source_y]
-            receive(("y", which, tag, way), ref)
+            ref = gath.at[which, plane, source_y]
+            receive(("own", which, way), ref)
             piece = ref.at[:, pl.ds(column, HALF)]
-            send(("half", which, tag, way), piece, piece, target)
-
-    def gather_done(which, tag):
-        for way in range(2):
-            column = ways[way][2]
-            piece = gath.at[which, planes[tag], y_far, :, pl.ds(column, HALF)]
-            receive(("half", which, tag, way), piece)
+            send(("own half", which, way), piece, piece, target)
+
+    def own_done(which):
+        for way in range(2):
+            piece = gath.at[which, plane, y_far, :, pl.ds(ways[way][2], HALF)]
+            receive(("own half", which, way), piece)
 
     def rows_of(chunk):
         return pl.ds(chunk * CHUNK, CHUNK)
@@ -207,7 +233,7 @@
     def sum_far(total, chunk, tag):
         for way in range(2):
             target, _, column = ways[way]
-            piece = part.at[total, planes[tag], y_far, rows_of(chunk), pl.ds(column, HALF)]
+            piece = part.at[total, planes[tag], y_far, chunk, :, pl.ds(column, HALF)]
             send(("part", total, chunk, tag, way), piece, halves.at[total, chunk, tag, way], target)
 
     def sum_near(total, chunk, tag):
@@ -216,19 +242,23 @@
             near = y_up if way == 0 else y_down
             landed = halves.at[total, chunk, tag, way]
             receive(("part", total, chunk, tag, way), landed)
-            piece = (total, planes[tag], near, rows_of(chunk), pl.ds(column, HALF))
+            piece = (total, planes[tag], near, chunk, slice(None), pl.ds(column, HALF))
             part[piece] = (part[piece].astype(F32) + landed[...].astype(F32)).astype(BF16)
             send(
                 ("pair", total, chunk, tag, way),
-                part.at[total, planes[tag], near, rows_of(chunk)],
+                part.at[total, planes[tag], near, chunk],
                 pairs.at[total, chunk, tag, way],
                 target,
             )
 
+    def near(total, chunk):
+        sum_near(total, chunk, 1)
+        sum_near(total, chunk, 0)
+
     def plane_sum(total, chunk, tag):
         for way in range(2):
             receive(("pair", total, chunk, tag, way), pairs.at[total, chunk, tag, way])
-        own = part[total, planes[tag], y, rows_of(chunk)].astype(F32)
+        own = part[total, planes[tag], y, chunk].astype(F32)
         return (
             own
             + pairs[total, chunk, tag, 0].astype(F32)
@@ -247,15 +277,6 @@
     def normed(values):
         factor = lax.rsqrt(jnp.mean(values * values, axis=-1, keepdims=True) + EPSILON)
         return (values * factor * gain_v[...]).astype(BF16)
-
-    local["act"].wait()
-    local["gain"].wait()
-    gath[NOW, plane, y] = normed(act_v[...].astype(F32))
-    local["up"].wait()
-    pl.semaphore_wait(barrier, len(peers))
-    gather_z(NOW)
-    gather_y(UP, 0)
-    gather_y(NOW, 0)
 
     local["marks"].wait()
     marked = jnp.where(marks_v[...] == 1, 1.0, 0.0).astype(BF16)
@@ -281,10 +302,15 @@
     far_moved, far_pack, far_unpack = selection(sections - 1 - section)
     local["guest"].wait()
     pack_send[0] = dot(far_pack, guest_v[...]).astype(BF16)
+    local["act"].wait()
+    local["gain"].wait()
+    gath[NOW, plane, y] = normed(act_v[...].astype(F32))
+    local["up"].wait()
+    pl.semaphore_wait(barrier, len(peers))
     send(("guest",), pack_send.at[0], pack_recv.at[0], to_mirror)
-    gather_z(UP)
+    own_send(UP)
+    own_send(NOW)
     pack_send[1] = dot(own_pack, act_v[...]).astype(BF16)
-    send(("leave",), pack_send.at[1], pack_recv.at[1], to_mirror)
     kept_v[...] = jnp.where(own_moved, 0.0, act_v[...].astype(F32)).astype(BF16)
     kept_copy = pltpu.make_async_copy(kept_v, kept_out, local_sem.at[9])
     kept_copy.start()
@@ -305,28 +331,31 @@
 
     lax.fori_loop(0, WIDTH // HEAD_DIM, split_rows, 0)
 
-    gather_forward(UP, 0)
+    own_forward(UP)
+    receive(("guest",), pack_recv.at[0])
+    cross(NOW, 0)
+    cross(NOW, 1)
     local["stash"].wait()
-    receive(("guest",), pack_recv.at[0])
     returned = dot(own_unpack, pack_recv[0])
     back_rows = jnp.where(own_moved, returned, stash_v[...].astype(F32))
     back_v[...] = back_rows.astype(BF16)
     gath[BACK, plane, y] = normed(back_rows)
-    gather_y(BACK, 0)
-    gather_z(BACK)
-    gather_forward(NOW, 0)
-    receive(("leave",), pack_recv.at[1])
-    held_v[...] = dot(far_unpack, pack_recv[1]).astype(BF16)
-    held_copy = pltpu.make_async_copy(held_v, held_out, local_sem.at[10])
-    held_copy.start()
-    gather_z_done(NOW)
-    gather_y(NOW, 1)
-    gather_forward(BACK, 0)
-    gather_z_done(UP)
-    gather_y(UP, 1)
-    gather_forward(NOW, 1)
-    gather_done(NOW, 0)
-    gather_done(NOW, 1)
+    own_send(BACK)
+    own_forward(NOW)
+    crossed(NOW, 0)
+    cross(BACK, 0)
+    crossed(NOW, 1)
+    cross(BACK, 1)
+    own_forward(BACK)
+    far_forward(NOW, 0)
+    far_forward(NOW, 1)
+    crossed(BACK, 0)
+    cross(UP, 0)
+    crossed(BACK, 1)
+    cross(UP, 1)
+    own_done(UP)
+    own_done(NOW)
+    far_done(NOW)
     local["query"].wait()
 
     def project(which):
@@ -348,9 +377,9 @@
         return raised / jnp.sum(raised, axis=-1, keepdims=True)
 
     project(NOW)
-    gather_z_done(BACK)
-    gather_y(BACK, 1)
-    gather_forward(UP, 1)
+    far_forward(BACK, 0)
+    far_forward(BACK, 1)
+    crossed(UP, 0)
 
     keys_now = qkv[0, :, QCOLS : QCOLS + HEAD_DIM]
     values_now = qkv[0, :, QCOLS + HEAD_DIM :]
@@ -359,23 +388,29 @@
         weights = probabilities(qkv[0, :, columns], keys_now).astype(BF16)
         context[:, columns] = dot(weights, values_now).astype(BF16)
 
+    crossed(UP, 1)
+    send(("leave",), pack_send.at[1], pack_recv.at[1], to_mirror)
     local["output"].wait()
 
     def forward_tile(step, carry):
         columns = pl.ds(pl.multiple_of(step * 512, 512), 512)
-        result = dot(context[...], wout[:, columns]).astype(BF16)
-        part[0, :, :, :, columns] = result.reshape(2, 4, ROWS, 512)
+        result = dot(context[...], wout[:, columns]).reshape(2, 4, CHUNKS, CHUNK, 512)
+        part[0, :, :, :, :, columns] = result.astype(BF16)
         return carry
 
     lax.fori_loop(0, WIDTH // 512, forward_tile, 0)
 
-    gather_forward(BACK, 1)
     for chunk in range(CHUNKS):
         for tag in (1, 0):
             sum_far(0, chunk, tag)
-
-    gather_done(UP, 0)
-    gather_done(UP, 1)
+    far_forward(UP, 0)
+    far_forward(UP, 1)
+    own_done(BACK)
+    far_done(BACK)
+    project(BACK)
+    for chunk in range(CHUNKS):
+        near(0, chunk)
+    far_done(UP)
 
     def grad_tile(step, carry):
         columns = pl.ds(pl.multiple_of(step * 256, 256), 256)
@@ -384,14 +419,6 @@
         return carry
 
     lax.fori_loop(0, QCOLS // 256, grad_tile, 0)
-
-    gather_done(BACK, 0)
-    gather_done(BACK, 1)
-    sum_near(0, 0, 1)
-    sum_near(0, 0, 0)
-    project(BACK)
-    sum_near(0, 1, 1)
-    sum_near(0, 1, 0)
 
     keys_back = qkv[1, :, QCOLS : QCOLS + HEAD_DIM]
     values_back = qkv[1, :, QCOLS + HEAD_DIM :]
@@ -411,29 +438,40 @@
     gcat[:, QCOLS : QCOLS + HEAD_DIM] = grad_key.astype(BF16)
     gcat[:, QCOLS + HEAD_DIM :] = grad_value.astype(BF16)
 
+    receive(("leave",), pack_recv.at[1])
+    held_v[...] = dot(far_unpack, pack_recv[1]).astype(BF16)
+    held_copy = pltpu.make_async_copy(held_v, held_out, local_sem.at[10])
+    held_copy.start()
     sum_cross(0, 0)
-
-    for chunk in range(CHUNKS):
-        grads = gcat[...].reshape(8, ROWS, CCOLS)[:, chunk * CHUNK : (chunk + 1) * CHUNK]
-        grads = grads.reshape(8 * CHUNK, CCOLS)
+    sum_cross(0, 1)
+
+    stage_rows = ROWS // STAGES
+    stage_chunks = CHUNKS // STAGES
+    for stage in range(STAGES):
+        grads = gcat[...].reshape(8, ROWS, CCOLS)[:, stage * stage_rows : (stage + 1) * stage_rows]
+        grads = grads.reshape(8 * stage_rows, CCOLS)
+
+        stage_chunk = pl.ds(stage * stage_chunks, stage_chunks)
 
         def backward_tile(step, carry):
             columns = pl.ds(pl.multiple_of(step * 512, 512), 512)
-            result = dot_last(grads, wcat[columns, :]).astype(BF16)
-            part[1, :, :, rows_of(chunk), columns] = result.reshape(2, 4, CHUNK, 512)
+            result = dot_last(grads, wcat[columns, :]).reshape(2, 4, stage_chunks, CHUNK, 512)
+            part[1, :, :, stage_chunk, :, columns] = result.astype(BF16)
             return carry
 
         lax.fori_loop(0, WIDTH // 512, backward_tile, 0)
-        for tag in (1, 0):
-            sum_far(1, chunk, tag)
-
-    sum_cross(0, 1)
+        for chunk in range(stage * stage_chunks, (stage + 1) * stage_chunks):
+            for tag in (1, 0):
+                sum_far(1, chunk, tag)
+
+    sum_cross(0, 2)
+    sum_cross(0, 3)
 
     def finish_forward(chunk):
         rows = rows_of(chunk)
         total = sum_total(0, chunk)
-        shift_v[0, rows] = (act_v[rows, :].astype(F32) + total).astype(BF16)
-        send(("shift", 0, chunk), shift_v.at[0, rows], next_out.at[rows], to_next)
+        shift_v[0, chunk] = (act_v[rows, :].astype(F32) + total).astype(BF16)
+        send(("shift", 0, chunk), shift_v.at[0, chunk], next_out.at[rows], to_next)
 
     def finish_backward(chunk):
         rows = rows_of(chunk)
@@ -443,19 +481,18 @@
         grads = sum_total(1, chunk) * gain_v[...]
         inner = jnp.sum(grads * values, axis=-1, keepdims=True) * (factor * factor * factor)
         norm_grad = grads * factor - values * (inner * (1.0 / WIDTH))
-        shift_v[1, rows] = (upstream + norm_grad).astype(BF16)
-        send(("shift", 1, chunk), shift_v.at[1, rows], prev_out.at[rows], to_prev)
-
-    sum_near(1, 0, 1)
-    sum_near(1, 0, 0)
-    finish_forward(0)
-    sum_near(1, 1, 1)
-    sum_near(1, 1, 0)
-    finish_forward(1)
-    sum_cross(1, 0)
-    sum_cross(1, 1)
-    finish_backward(0)
-    finish_backward(1)
+        shift_v[1, chunk] = (upstream + norm_grad).astype(BF16)
+        send(("shift", 1, chunk), shift_v.at[1, chunk], prev_out.at[rows], to_prev)
+
+    for chunk in range(CHUNKS):
+        near(1, chunk)
+    for chunk in range(CHUNKS):
+        finish_forward(chunk)
+    for chunk in range(CHUNKS):
+        sum_cross(1, chunk)
+        if chunk > 0:
+            finish_backward(chunk - 1)
+    finish_backward(CHUNKS - 1)
 
     kept_copy.wait()
     held_copy.wait()
@@ -478,7 +515,7 @@
         out_specs=(anywhere,) * 4,
         scratch_shapes=[
             vmem((3, 2, 4, ROWS, WIDTH), BF16),
-            vmem((2, 2, 4, ROWS, WIDTH), BF16),
+            vmem((2, 2, 4, CHUNKS, CHUNK, WIDTH), BF16),
             vmem((2, CHUNKS, 2, 2, CHUNK, HALF), BF16),
             vmem((2, CHUNKS, 2, 2, CHUNK, WIDTH), BF16),
             vmem((2, CHUNKS, CHUNK, WIDTH), BF16),
@@ -500,7 +537,7 @@
             vmem((2, PACKED, WIDTH), BF16),
             vmem((ROWS, WIDTH), BF16),
             vmem((ROWS, WIDTH), BF16),
-            vmem((2, ROWS, WIDTH), BF16),
+            vmem((2, CHUNKS, CHUNK, WIDTH), BF16),
             pltpu.SemaphoreType.DMA((count,)),
             pltpu.SemaphoreType.DMA((count,)),
             pltpu.SemaphoreType.DMA((11,)),
@@ -534,10 +571,17 @@
         output_weight[0],
         evict_marks.T,
     )
-    next_input = jnp.where(section == 0, jnp.zeros_like(next_raw), next_raw)
     last = lax.axis_size("section") - 1
-    prev_grad = jnp.where(section == last, jnp.zeros_like(prev_raw), prev_raw)
-    return (next_input[None], prev_grad[None], kept[None], held[None])
+
+    def unless(empty, rows):
+        return jnp.where(empty, jnp.zeros_like(rows), rows)[None]
+
+    return (
+        unless(section == 0, next_raw),
+        unless(section == last, prev_raw),
+        unless(section > last, kept),
+        unless(section > last, held),
+    )
 
 
 def solution(mesh):

time: 142 us -> 120 us (0.85)
  Pallas kernels: 136 us -> 116 us
  local copies, waits for them, and re-layouts: 3.34 us -> 0 us
  other arithmetic: 1.87 us -> 3.72 us
    pallas_call x1, Pallas kernels: 136 us -> 116 us  [relay(): pl.pallas_call(relay_kernel, out_shape=(block, block, block, block), in_s...]
    unnamed x2 -> x0, local copies, waits for them, and re-layouts: 3.34 us -> none
    broadcast_in_dim x1 -> x2, other arithmetic: 1.87 us -> 3.72 us  [unless(): return jnp.where(empty, jnp.zeros_like(rows), rows)[None]]
where the time goes in v2:
time: 120 us
  Pallas kernels  116 us (97%)
  other arithmetic  3.72 us (3%)
    pallas_call x1, Pallas kernels, relay(): pl.pallas_call(relay_kernel, out_shape=(block, block, block, block), in_s...  116 us
    broadcast_in_dim x2, other arithmetic, unless(): return jnp.where(empty, jnp.zeros_like(rows), rows)[None]  3.72 us

profile of v2, /device:TPU:1, one launch (start us, length us, event | category | flops | bytes accessed | tf_op | source)
XLA Modules:
  0.0 119.9 jit_solution(7993754348527476063)
XLA Ops:
  0.6 115.5 %shard_map.120 = (bf16[32,4096]{1,0:T(8,128)(2,1)}, bf16[32,4096]{1,0:T(8,128)(2,1)}, bf16[32,4096]{1,0:T(8,128)(2,1)}, bf16[32,4096]{1,0:T(8,128)(2,1)}) custom-call(bf16[32,4096]{1,0:T(8,128)(2,1)} %bitcast.19, bf16[32,4096]{1,0:T(8,128)(2,1)} %bitcast.20, bf16[32,4096]{1,0:T(8,128)(2,1)} %bitcast.21, bf16[32,4096]{1,0:T(8,128)(2,1)} %bitcast.22, ...), custom_call_target="tpu_custom_call" | custom-call | tf_op jit(solution)/shard_map/pallas_call | solution.py:511
  116.2 1.9 %select_bitcast_fusion.2 = (bf16[1,32,4096]{2,1,0:T(8,128)(2,1)}, bf16[1,32,4096]{2,1,0:T(8,128)(2,1)}) fusion(bf16[32,4096]{1,0:T(8,128)(2,1)} %get-tuple-element.9, pred[]{:T(512)S(6)} %eq.7, bf16[32,4096]{1,0:T(8,128)(2,1)} %get-tuple-element.8, pred[]{:T(512)S(6)} %eq.6), kind=kLoop, calls=%fused_computation.2 | loop fusion | flops 262144 | bytes 1048578 | tf_op jit(solution)/shard_map/broadcast_in_dim | solution.py:577
  118.0 1.9 %select_bitcast_fusion = (bf16[1,32,4096]{2,1,0:T(8,128)(2,1)}, bf16[1,32,4096]{2,1,0:T(8,128)(2,1)}) fusion(bf16[32,4096]{1,0:T(8,128)(2,1)} %get-tuple-element.11, pred[]{:T(512)S(6)} %gt.4, bf16[32,4096]{1,0:T(8,128)(2,1)} %get-tuple-element.10), kind=kLoop, calls=%fused_computation | loop fusion | flops 262144 | bytes 1048577 | tf_op jit(solution)/shard_map/broadcast_in_dim | solution.py:577

commit v3 on v2

--- a/solution.py
+++ b/solution.py
@@ -18,7 +18,7 @@
 ROWS = 32
 WIDTH = 4096
 HALF = WIDTH // 2
-QUARTER = WIDTH // 4
+PIECE = ROWS // 2
 BLOCKS = 16
 PACKED = 16
 CHUNKS = 4
@@ -47,8 +47,11 @@
                 for way in range(2):
                     names.append(("part", total, chunk, tag, way))
                     names.append(("pair", total, chunk, tag, way))
-            names.append(("sum", total, chunk))
+            if total == 0:
+                names.append(("sum", total, chunk))
             names.append(("shift", total, chunk))
+    for chunk in range(CHUNKS):
+        names.append(("shift far", chunk))
     names.append(("guest",))
     names.append(("leave",))
     return {name: number for number, name in enumerate(names)}
@@ -85,6 +88,7 @@
     marks_in,
     next_out,
     prev_out,
+    prev_far_out,
     held_out,
     kept_out,
     gath,
@@ -97,6 +101,7 @@
     stash_v,
     guest_v,
     back_v,
+    far_back_v,
     gain_v,
     marks_v,
     kv_mixed,
@@ -133,7 +138,9 @@
     to_mirror = at(sections - 1 - section, tensor)
     to_next = at((section + 1) % sections, tensor)
     to_prev = at((section + sections - 1) % sections, tensor)
-    peers = (to_up, to_down, to_far_z, to_mirror, to_next, to_prev)
+    to_prev_far = at((section + sections - 1) % sections, (1 - plane) * 4 + y)
+    from_next_far = at((section + 1) % sections, (1 - plane) * 4 + y)
+    peers = (to_up, to_down, to_far_z, to_mirror, to_next, to_prev, to_prev_far, from_next_far)
 
     barrier = pltpu.get_barrier_semaphore()
     for peer in peers:
@@ -180,34 +187,43 @@
     planes = (plane, 1 - plane)
     ways = ((to_up, y_down, 0), (to_down, y_up, HALF))
 
-    def columns_of(piece):
-        return pl.ds(piece * HALF, HALF)
+    def piece_rows(piece):
+        return pl.ds(piece * PIECE, PIECE)
 
     def cross(which, piece):
-        ref = gath.at[which, plane, y, :, columns_of(piece)]
-        send(("z", which, piece), ref, ref, to_far_z)
+        rows = piece_rows(piece)
+        if which == BACK:
+            source, target = back_v.at[rows], far_back_v.at[rows]
+        else:
+            source = gath.at[which, plane, y, rows]
+            target = source
+        send(("z", which, piece), source, target, to_far_z)
 
     def crossed(which, piece):
-        receive(("z", which, piece), gath.at[which, 1 - plane, y, :, columns_of(piece)])
-        ref = gath.at[which, 1 - plane, y, :, columns_of(piece)]
+        rows = piece_rows(piece)
+        ref = gath.at[which, 1 - plane, y, rows]
+        if which == BACK:
+            receive(("z", which, piece), far_back_v.at[rows])
+            gath[which, 1 - plane, y, rows] = normed(far_back_v[rows, :].astype(F32))
+        else:
+            receive(("z", which, piece), ref)
         for way in range(2):
             send(("far", which, piece, way), ref, ref, ways[way][0])
 
     def far_forward(which, piece):
         for way in range(2):
-            target, source_y, _ = ways[way]
-            ref = gath.at[which, 1 - plane, source_y]
-            receive(("far", which, piece, way), ref.at[:, columns_of(piece)])
-            part_ref = ref.at[:, pl.ds(piece * HALF + way * QUARTER, QUARTER)]
+            target, source_y, column = ways[way]
+            ref = gath.at[which, 1 - plane, source_y, piece_rows(piece)]
+            receive(("far", which, piece, way), ref)
+            part_ref = ref.at[:, pl.ds(column, HALF)]
             send(("far half", which, piece, way), part_ref, part_ref, target)
 
     def far_done(which):
         for piece in range(2):
             for way in range(2):
-                columns = pl.ds(piece * HALF + way * QUARTER, QUARTER)
-                receive(
-                    ("far half", which, piece, way), gath.at[which, 1 - plane, y_far, :, columns]
-                )
+                columns = pl.ds(ways[way][2], HALF)
+                ref = gath.at[which, 1 - plane, y_far, piece_rows(piece), columns]
+                receive(("far half", which, piece, way), ref)
 
     def own_send(which):
         ref = gath.at[which, plane, y]
@@ -473,26 +489,34 @@
         shift_v[0, chunk] = (act_v[rows, :].astype(F32) + total).astype(BF16)
         send(("shift", 0, chunk), shift_v.at[0, chunk], next_out.at[rows], to_next)
 
-    def finish_backward(chunk):
+    def norm_grad(values, total):
+        factor = lax.rsqrt(jnp.mean(values * values, axis=-1, keepdims=True) + EPSILON)
+        grads = total * gain_v[...]
+        inner = jnp.sum(grads * values, axis=-1, keepdims=True) * (factor * factor * factor)
+        return grads * factor - values * (inner * (1.0 / WIDTH))
+
+    def finish_far(chunk):
         rows = rows_of(chunk)
-        values = back_v[rows, :].astype(F32)
-        factor = lax.rsqrt(jnp.mean(values * values, axis=-1, keepdims=True) + EPSILON)
+        grad = norm_grad(far_back_v[rows, :].astype(F32), plane_sum(1, chunk, 1))
+        zsend[1, chunk] = grad.astype(BF16)
+        send(("shift far", chunk), zsend.at[1, chunk], prev_far_out.at[rows], to_prev_far)
+
+    def finish_own(chunk):
+        rows = rows_of(chunk)
+        grad = norm_grad(back_v[rows, :].astype(F32), plane_sum(1, chunk, 0))
         upstream = gath[UP, plane, y, rows].astype(F32)
-        grads = sum_total(1, chunk) * gain_v[...]
-        inner = jnp.sum(grads * values, axis=-1, keepdims=True) * (factor * factor * factor)
-        norm_grad = grads * factor - values * (inner * (1.0 / WIDTH))
-        shift_v[1, chunk] = (upstream + norm_grad).astype(BF16)
+        shift_v[1, chunk] = (upstream + grad).astype(BF16)
         send(("shift", 1, chunk), shift_v.at[1, chunk], prev_out.at[rows], to_prev)
 
-    for chunk in range(CHUNKS):
-        near(1, chunk)
+    for tag in (1, 0):
+        for chunk in range(CHUNKS):
+            sum_near(1, chunk, tag)
     for chunk in range(CHUNKS):
         finish_forward(chunk)
     for chunk in range(CHUNKS):
-        sum_cross(1, chunk)
-        if chunk > 0:
-            finish_backward(chunk - 1)
-    finish_backward(CHUNKS - 1)
+        finish_far(chunk)
+    for chunk in range(CHUNKS):
+        finish_own(chunk)
 
     kept_copy.wait()
     held_copy.wait()
@@ -501,6 +525,7 @@
     for chunk in range(CHUNKS):
         receive(("shift", 0, chunk), next_out.at[rows_of(chunk)])
         receive(("shift", 1, chunk), prev_out.at[rows_of(chunk)])
+        receive(("shift far", chunk), prev_far_out.at[rows_of(chunk)])
 
 
 def relay(act, up, stash, guest, gain, query, keyval, output, marks):
@@ -510,9 +535,9 @@
     vmem = pltpu.VMEM
     return pl.pallas_call(
         relay_kernel,
-        out_shape=(block, block, block, block),
+        out_shape=(block,) * 5,
         in_specs=[anywhere] * 9,
-        out_specs=(anywhere,) * 4,
+        out_specs=(anywhere,) * 5,
         scratch_shapes=[
             vmem((3, 2, 4, ROWS, WIDTH), BF16),
             vmem((2, 2, 4, CHUNKS, CHUNK, WIDTH), BF16),
@@ -520,6 +545,7 @@
             vmem((2, CHUNKS, 2, 2, CHUNK, WIDTH), BF16),
             vmem((2, CHUNKS, CHUNK, WIDTH), BF16),
             vmem((2, CHUNKS, CHUNK, WIDTH), BF16),
+            vmem((ROWS, WIDTH), BF16),
             vmem((ROWS, WIDTH), BF16),
             vmem((ROWS, WIDTH), BF16),
             vmem((ROWS, WIDTH), BF16),
@@ -548,6 +574,70 @@
     )(act, up, stash, guest, gain, query, keyval, output, marks)
 
 
+def finish_kernel(
+    next_in,
+    prev_in,
+    prev_far_in,
+    held_in,
+    kept_in,
+    next_out,
+    prev_out,
+    kept_out,
+    held_out,
+    next_v,
+    prev_v,
+    prev_far_v,
+    held_v,
+    kept_v,
+    sem,
+):
+    section = lax.axis_index("section")
+    arrivals = (
+        (next_in, next_v),
+        (prev_in, prev_v),
+        (prev_far_in, prev_far_v),
+        (held_in, held_v),
+        (kept_in, kept_v),
+    )
+    loads = []
+    for number, (source, target) in enumerate(arrivals):
+        loads.append(pltpu.make_async_copy(source, target, sem.at[number]))
+        loads[-1].start()
+    stores = []
+
+    def store(source, target):
+        stores.append(pltpu.make_async_copy(source, target, sem.at[5 + len(stores)]))
+        stores[-1].start()
+
+    loads[0].wait()
+    next_v[...] = jnp.where(section == 0, 0.0, next_v[...].astype(F32)).astype(BF16)
+    store(next_v, next_out)
+    loads[1].wait()
+    loads[2].wait()
+    total = prev_v[...].astype(F32) + prev_far_v[...].astype(F32)
+    prev_v[...] = jnp.where(section == 31, 0.0, total).astype(BF16)
+    store(prev_v, prev_out)
+    loads[3].wait()
+    store(held_v, held_out)
+    loads[4].wait()
+    store(kept_v, kept_out)
+    for copy in stores:
+        copy.wait()
+
+
+def finish(*raw):
+    block = jax.ShapeDtypeStruct((ROWS, WIDTH), BF16)
+    anywhere = pl.BlockSpec(memory_space=pl.ANY)
+    return pl.pallas_call(
+        finish_kernel,
+        out_shape=(block,) * 4,
+        in_specs=[anywhere] * 5,
+        out_specs=(anywhere,) * 4,
+        scratch_shapes=[pltpu.VMEM((ROWS, WIDTH), BF16)] * 5 + [pltpu.SemaphoreType.DMA((9,))],
+        compiler_params=pltpu.CompilerParams(vmem_limit_bytes=60 * 2**20),
+    )(*raw)
+
+
 def local(
     activations,
     upstream_grad,
@@ -559,8 +649,7 @@
     output_weight,
     evict_marks,
 ):
-    section = lax.axis_index("section")
-    next_raw, prev_raw, held, kept = relay(
+    raw = relay(
         activations[0],
         upstream_grad[0],
         stash_blocks[0],
@@ -571,17 +660,7 @@
         output_weight[0],
         evict_marks.T,
     )
-    last = lax.axis_size("section") - 1
-
-    def unless(empty, rows):
-        return jnp.where(empty, jnp.zeros_like(rows), rows)[None]
-
-    return (
-        unless(section == 0, next_raw),
-        unless(section == last, prev_raw),
-        unless(section > last, kept),
-        unless(section > last, held),
-    )
+    return tuple(rows[None] for rows in finish(*raw))
 
 
 def solution(mesh):

time: 120 us -> 113 us (0.942)
  Pallas kernels: 116 us -> 111 us
  other arithmetic: 3.72 us -> 0 us
    pallas_call x1 -> x2, Pallas kernels: 116 us -> 111 us  [the longest x1 109 us: relay(): pl.pallas_call(relay_kernel, out_shape=(block,) * 5, in_specs=[anywhere]...]
    broadcast_in_dim x2 -> x0, other arithmetic: 3.72 us -> none  [unless(): return jnp.where(empty, jnp.zeros_like(rows), rows)[None]]
where the time goes in v3:
time: 113 us; the launch traced here: 112 us
  Pallas kernels  111 us (98%)
    pallas_call x1, Pallas kernels, relay(): pl.pallas_call(relay_kernel, out_shape=(block,) * 5, in_specs=[anywhere]...  109 us

profile of v3, /device:TPU:1, one launch (start us, length us, event | category | flops | bytes accessed | tf_op | source)
XLA Modules:
  0.0 111.9 jit_solution(4936521434015080877)
XLA Ops:
  0.6 109.1 %shard_map.120 = (bf16[32,4096]{1,0:T(8,128)(2,1)}, bf16[32,4096]{1,0:T(8,128)(2,1)}, bf16[32,4096]{1,0:T(8,128)(2,1)}, bf16[32,4096]{1,0:T(8,128)(2,1)}, bf16[32,4096]{1,0:T(8,128)(2,1)}) custom-call(bf16[32,4096]{1,0:T(8,128)(2,1)} %bitcast.15, bf16[32,4096]{1,0:T(8,128)(2,1)} %bitcast.16, bf16[32,4096]{1,0:T(8,128)(2,1)} %bitcast.17, ...), custom_call_target="tpu_custom_call" | custom-call | tf_op jit(solution)/shard_map/pallas_call | solution.py:536
  109.7 2.1 %shard_map.121 = (bf16[32,4096]{1,0:T(8,128)(2,1)}, bf16[32,4096]{1,0:T(8,128)(2,1)}, bf16[32,4096]{1,0:T(8,128)(2,1)}, bf16[32,4096]{1,0:T(8,128)(2,1)}) custom-call(bf16[32,4096]{1,0:T(8,128)(2,1)} %get-tuple-element.13.next_in, bf16[32,4096]{1,0:T(8,128)(2,1)} %get-tuple-element.14.prev_in, bf16[32,4096]{1,0:T(8,128)(2,1)} %get-tuple-element.15.prev_far_in, ...), custom_call_target="tpu_custom_call" | custom-call | tf_op jit(solution)/shard_map/pallas_call | solution.py:631

commit v4 on v3

--- a/solution.py
+++ b/solution.py
@@ -476,8 +476,8 @@
             return carry
 
         lax.fori_loop(0, WIDTH // 512, backward_tile, 0)
-        for chunk in range(stage * stage_chunks, (stage + 1) * stage_chunks):
-            for tag in (1, 0):
+        for tag in (1, 0):
+            for chunk in range(stage * stage_chunks, (stage + 1) * stage_chunks):
                 sum_far(1, chunk, tag)
 
     sum_cross(0, 2)

time: 113 us -> 113 us (level)
  no operation moved by 1% of the time
where the time goes in v4:
time: 113 us; the launch traced here: 112 us
  Pallas kernels  111 us (98%)
    pallas_call x1, Pallas kernels, relay(): pl.pallas_call(relay_kernel, out_shape=(block,) * 5, in_specs=[anywhere]...  109 us

profile of v4, /device:TPU:1, one launch (start us, length us, event | category | flops | bytes accessed | tf_op | source)
XLA Modules:
  0.0 111.9 jit_solution(7370621915672410722)
XLA Ops:
  0.6 109.1 %shard_map.120 = (bf16[32,4096]{1,0:T(8,128)(2,1)}, bf16[32,4096]{1,0:T(8,128)(2,1)}, bf16[32,4096]{1,0:T(8,128)(2,1)}, bf16[32,4096]{1,0:T(8,128)(2,1)}, bf16[32,4096]{1,0:T(8,128)(2,1)}) custom-call(bf16[32,4096]{1,0:T(8,128)(2,1)} %bitcast.15, bf16[32,4096]{1,0:T(8,128)(2,1)} %bitcast.16, bf16[32,4096]{1,0:T(8,128)(2,1)} %bitcast.17, ...), custom_call_target="tpu_custom_call" | custom-call | tf_op jit(solution)/shard_map/pallas_call | solution.py:536
  109.7 2.1 %shard_map.121 = (bf16[32,4096]{1,0:T(8,128)(2,1)}, bf16[32,4096]{1,0:T(8,128)(2,1)}, bf16[32,4096]{1,0:T(8,128)(2,1)}, bf16[32,4096]{1,0:T(8,128)(2,1)}) custom-call(bf16[32,4096]{1,0:T(8,128)(2,1)} %get-tuple-element.13.next_in, bf16[32,4096]{1,0:T(8,128)(2,1)} %get-tuple-element.14.prev_in, bf16[32,4096]{1,0:T(8,128)(2,1)} %get-tuple-element.15.prev_far_in, ...), custom_call_target="tpu_custom_call" | custom-call | tf_op jit(solution)/shard_map/pallas_call | solution.py:631
